TPU v7x, 32 devices: a whole 2x2x4 slice. The times are simulated.
32 devices in a mesh: dap: 8 (over y, x, core), seq: 4 (over z).
Axes of the slice: x: 2, y: 2, z: 4, core: 2. Of those that a mesh axis runs over, the one named last changes fastest.
Arguments:
- homolog_tensor: bfloat16 [8, 32, 256], P('dap', 'seq'), may hold values from -6 to 6
- pair_features: bfloat16 [32, 32, 128], P('seq', 'dap'), may hold values from -6 to 6
- entry_real_mask: int32 [8, 32], P('dap', 'seq'), may hold values 0 or 1
- chain_ids: int32 [32], replicated, may hold values from 0 to 3, never falling along the last dimension, each value on 1 to 16 neighbouring positions
- horizontal_matrices: bfloat16 [256, 1024], replicated, may hold values from -0.375 to 0.375
- horizontal_projector: bfloat16 [256, 256], replicated, may hold values from -0.375 to 0.375
- bias_proj: float32 [128, 8], replicated, may hold values from -35.35534 to 35.35534
- chain_bias: float32 [2, 8], replicated, may hold values from -4 to 4
- column_proj: bfloat16 [256, 1024], replicated, may hold values from -12.5 to 12.5
- vertical_projector: bfloat16 [256, 256], replicated, may hold values from -0.375 to 0.375
- expansion_matrix: bfloat16 [256, 1024], replicated, may hold values from -0.375 to 0.375
- contraction_matrix: bfloat16 [1024, 256], replicated, may hold values from -0.1875 to 0.1875
Outputs:
- updated: bfloat16 [8, 32, 256], P('dap', 'seq')
Inputs may be any that keep to these rules, and one draw needn't show every extreme that they name: `chain_ids`: chain numbers never fall along the residues.
All inputs are finite; a program needn't handle non-finite values. No bound on the sum of `entry_real_mask` on one device may be relied on, other than what follows from the above.
Results may differ from a plain program's by a relative error of at most 0.013.
The roundings to bfloat16 on the way count: a program that leaves them out, or rounds other values in their place, can miss the bound.
Values may be sent and summed in bfloat16 or wider, within the bound.
No kernel may reach another device: no remote copies, remote signals or barrier semaphores. Data moves between devices by JAX's collectives and lax.ppermute only.
A program may use at most 64 MiB of HBM per device.

v0:
```python
import jax
import jax.numpy as jnp
from jax import lax
from jax.sharding import PartitionSpec as P

HEAD_TOTAL = 8
HEAD_DEPTH = 32
epsilon = 1e-05


def layer_norm(inputs):
    center = inputs - jnp.mean(inputs, axis=-1, keepdims=True)
    spread = jnp.mean(center * center, axis=-1, keepdims=True)
    return center * lax.rsqrt(spread + epsilon)


def attend(queries, key_part, value_part, keep_mask, bias_term):
    scores = jnp.einsum(
        "ihd,jhd->hij", queries, key_part, preferred_element_type=jnp.float32
    ) * HEAD_DEPTH ** (-0.5)
    if bias_term is not None:
        scores = scores + bias_term.astype(jnp.float32)
    scores = jnp.where(keep_mask[None, None, :] > 0, scores, -1000000000.0)
    weights = jax.nn.softmax(scores, axis=-1).astype(jnp.bfloat16)
    return jnp.einsum("hij,jhd->ihd", weights, value_part, preferred_element_type=jnp.float32)


def column_update(
    column, keep_column, column_proj, vertical_projector, expansion_matrix, contraction_matrix
):
    expanded_dimension = HEAD_TOTAL * HEAD_DEPTH
    standardized = layer_norm(column.astype(jnp.float32)).astype(jnp.bfloat16)
    projected = jnp.dot(standardized, column_proj, preferred_element_type=jnp.float32).astype(
        jnp.bfloat16
    )
    queries = projected[:, :expanded_dimension].reshape(-1, HEAD_TOTAL, HEAD_DEPTH)
    key_part = projected[:, expanded_dimension : 2 * expanded_dimension].reshape(
        -1, HEAD_TOTAL, HEAD_DEPTH
    )
    value_part = projected[:, 2 * expanded_dimension : 3 * expanded_dimension].reshape(
        -1, HEAD_TOTAL, HEAD_DEPTH
    )
    attended = attend(queries, key_part, value_part, keep_column, None).reshape(
        -1, expanded_dimension
    )
    sigmoid_scaled = (
        jax.nn.sigmoid(projected[:, 3 * expanded_dimension :].astype(jnp.float32)) * attended
    ).astype(jnp.bfloat16)
    mixed = column.astype(jnp.float32) + jnp.dot(
        sigmoid_scaled, vertical_projector, preferred_element_type=jnp.float32
    )
    inner = jnp.maximum(
        jnp.dot(
            layer_norm(mixed).astype(jnp.bfloat16),
            expansion_matrix,
            preferred_element_type=jnp.float32,
        ),
        0.0,
    ).astype(jnp.bfloat16)
    return (mixed + jnp.dot(inner, contraction_matrix, preferred_element_type=jnp.float32)).astype(
        jnp.bfloat16
    )


def body(
    homolog_tensor,
    pair_features,
    entry_real_mask,
    chain_ids,
    horizontal_matrices,
    horizontal_projector,
    bias_proj,
    chain_bias,
    column_proj,
    vertical_projector,
    expansion_matrix,
    contraction_matrix,
):
    row_count, local_residues, channels = homolog_tensor.shape
    expanded_dimension = HEAD_TOTAL * HEAD_DEPTH
    dap_count = lax.axis_size("dap")
    pair_rows, pair_columns, pair_width = pair_features.shape
    normed_pair = layer_norm(pair_features.astype(jnp.float32))
    projected_pair = jnp.einsum(
        "ijc,ch->hij", normed_pair, bias_proj, precision=lax.Precision.HIGHEST
    )
    row_chain = lax.dynamic_slice_in_dim(chain_ids, lax.axis_index("seq") * pair_rows, pair_rows)
    column_chain = lax.dynamic_slice_in_dim(
        chain_ids, lax.axis_index("dap") * pair_columns, pair_columns
    )
    same_chain = (row_chain[:, None] == column_chain[None, :]).astype(jnp.float32)
    chain_term = chain_bias[0][:, None, None] * same_chain + chain_bias[1][:, None, None] * (
        1.0 - same_chain
    )
    local_bias = (projected_pair + chain_term).astype(jnp.bfloat16)
    pair_bias = lax.all_gather(local_bias, "dap", axis=2, tiled=True)
    standardized = layer_norm(homolog_tensor.astype(jnp.float32)).astype(jnp.bfloat16)
    flat = standardized.reshape(-1, channels)
    keep_mask = entry_real_mask.astype(jnp.bfloat16)
    projected = (
        jnp.dot(flat, horizontal_matrices, preferred_element_type=jnp.float32)
        .astype(jnp.bfloat16)
        .reshape(row_count, local_residues, 4 * expanded_dimension)
    )
    queries = projected[..., :expanded_dimension]
    gating = projected[..., 3 * expanded_dimension :]
    key_values, keep_all = (
        lax.all_gather(
            projected[..., expanded_dimension : 3 * expanded_dimension], "seq", axis=1, tiled=True
        ),
        lax.all_gather(keep_mask, "seq", axis=1, tiled=True),
    )

    def one_row(inputs_row):
        row_queries, row_pairs, row_keep = inputs_row
        key_part = row_pairs[:, :expanded_dimension].reshape(-1, HEAD_TOTAL, HEAD_DEPTH)
        value_part = row_pairs[:, expanded_dimension:].reshape(-1, HEAD_TOTAL, HEAD_DEPTH)
        return attend(
            row_queries.reshape(local_residues, HEAD_TOTAL, HEAD_DEPTH),
            key_part,
            value_part,
            row_keep,
            pair_bias,
        ).reshape(local_residues, expanded_dimension)

    attended = lax.map(one_row, (queries, key_values, keep_all))
    sigmoid_scaled = (jax.nn.sigmoid(gating.astype(jnp.float32)) * attended).astype(jnp.bfloat16)
    row_result = jnp.dot(
        sigmoid_scaled.reshape(-1, expanded_dimension),
        horizontal_projector,
        preferred_element_type=jnp.float32,
    ).reshape(row_count, local_residues, channels)
    updated_rows = (homolog_tensor.astype(jnp.float32) + row_result).astype(jnp.bfloat16)
    per_device = local_residues // dap_count
    blocks = updated_rows.reshape(row_count, dap_count, per_device, channels)
    keep_blocks = keep_mask.reshape(row_count, dap_count, per_device)

    def single_column(inputs_col):
        return column_update(
            inputs_col[0],
            inputs_col[1],
            column_proj,
            vertical_projector,
            expansion_matrix,
            contraction_matrix,
        )

    column_block = lax.all_to_all(blocks, "dap", split_axis=1, concat_axis=0, tiled=True)
    column_keep = lax.all_to_all(keep_blocks, "dap", split_axis=1, concat_axis=0, tiled=True)
    inputs_col = (jnp.moveaxis(column_block[:, 0], 1, 0), jnp.moveaxis(column_keep[:, 0], 1, 0))
    output_list = lax.map(single_column, inputs_col)
    mixed = jnp.moveaxis(output_list, 0, 1)[:, None]
    returned = lax.all_to_all(mixed, "dap", split_axis=0, concat_axis=1, tiled=True)
    return returned.reshape(row_count, local_residues, channels)


def solution(mesh):
    placed = (
        P("dap", "seq", None),
        P("seq", "dap", None),
        P("dap", "seq"),
        P(),
        P(),
        P(),
        P(),
        P(),
        P(),
        P(),
        P(),
        P(),
    )
    return jax.shard_map(
        body, mesh=mesh, in_specs=placed, out_specs=P("dap", "seq", None), check_vma=False
    )
```

profile of v0, /device:TPU:0, one launch (start us, length us, event | category | flops | bytes accessed | tf_op | source)
XLA Modules:
  0.0 71.7 jit_solution(17577258312015481253)
XLA Ops:
  0.0 0.7 convert_bitcast_fusion.1
  0.7 0.7 copy.49
  1.4 5.2 %all-to-all-start.1 = ((bf16[1,8,1]{2,0,1:T(2,128)(2,1)}), bf16[1,8,1]{2,0,1:T(2,128)(2,1)S(1)}, u32[]{:S(2)}, u32[]{:S(2)}) async-start(bf16[1,8,1]{2,0,1:T(2,128)(2,1)} %copy.49), calls=%async_computation.1 | async-start | bytes 8192 | tf_op jit(solution)/shard_map/all_to_all | solution.py:149
  6.6 0.7 copy-done.12
  7.6 0.5 copy-done.6
  8.3 0.2 fusion.12
  8.6 0.6 copy-done.7
  9.2 0.7 copy-done.5
  10.2 0.6 copy-done.9
  10.8 0.7 copy-done.11
  11.7 9.7 %all_gather.11 = bf16[8,8,32]{1,0,2:T(8,128)(2,1)S(1)} all-gather(bf16[8,8,4]{1,0,2:T(8,128)(2,1)S(1)} %copy.43), channel_id=1, replica_groups=mesh['dap'=8,'seq'=4] {'dap'}, dimensions={2}, use_global_device_ids=true | all-gather | bytes 4608 | tf_op jit(solution)/shard_map/all_gather | solution.py:96
  21.6 0.6 slice-done
  22.2 13.4 %all_gather.9 = bf16[1,32,512]{2,1,0:T(8,128)(2,1)S(1)} all-gather(bf16[1,8,512]{2,1,0:T(8,128)(2,1)S(1)} %slice-done), channel_id=1, replica_groups=mesh['dap'=8,'seq'=4] {'seq'}, dimensions={1}, use_global_device_ids=true | all-gather | bytes 40960 | tf_op jit(solution)/shard_map/all_gather | solution.py:108
  35.7 0.6 slice-done.1
  36.3 0.6 dynamic-slice
  37.6 0.2 dynamic-update-slice
  37.8 11.7 %all-reduce = bf16[32]{0:T(256)(128)(2,1)S(1)} all-reduce(bf16[32]{0:T(256)(128)(2,1)S(1)} %dynamic-update-slice), channel_id=1, replica_groups=mesh['dap'=8,'seq'=4] {'seq'}, use_global_device_ids=true, to_apply=%add | all-reduce | flops 32 | bytes 128
  50.0 0.3 convolution_bitcast_fusion.1
  50.3 0.5 copy-done.3
  51.2 0.6 broadcast.220
  51.8 0.7 %reduce.5 = bf16[8,256]{1,0:T(8,128)(2,1)S(1)} reduce(bf16[8,1,1,256]{3,2,1,0:T(2,128)(2,1)S(1)} %bitcast.75, bf16[]{:T(256)} %broadcast.220), dimensions={1,2}, to_apply=%bitcast.73.reduce_sub_computation | reduce | bytes 8194
  52.5 0.6 reshape.228
  53.1 3.3 %all-to-all-start = ((bf16[8,2,128]{2,1,0:T(2,128)(2,1)}), bf16[8,2,128]{2,1,0:T(2,128)(2,1)S(1)}, u32[]{:S(2)}, u32[]{:S(2)}) async-start(bf16[8,2,128]{2,1,0:T(2,128)(2,1)} %reshape.228), calls=%async_computation | async-start | bytes 8192 | tf_op jit(solution)/shard_map/all_to_all | solution.py:148
  56.4 0.2 compare_reduce_fusion
  56.6 4.3 %all-to-all-done = bf16[8,2,128]{2,1,0:T(2,128)(2,1)S(1)} async-done(((bf16[8,2,128]{2,1,0:T(2,128)(2,1)}), bf16[8,2,128]{2,1,0:T(2,128)(2,1)S(1)}, u32[]{:S(2)}, u32[]{:S(2)}) %all-to-all-start) | async-done | bytes 4128 | tf_op jit(solution)/shard_map/all_to_all | solution.py:148
  61.3 0.2 convolution_convert_fusion
  62.1 0.2 convolution_bitcast_fusion
  62.4 0.3 fusion.72
  62.9 0.4 fusion.18
  63.3 0.7 reduce.6
  64.0 7.1 %all_to_all.12 = bf16[8,2,128]{2,1,0:T(2,128)(2,1)S(1)} all-to-all(bf16[8,2,128]{2,1,0:T(2,128)(2,1)S(1)} %reshape.230), channel_id=1, replica_groups=mesh['dap'=8,'seq'=4] {'dap'}, dimensions={0} | all-to-all | bytes 8192 | tf_op jit(solution)/shard_map/all_to_all | solution.py:153
  71.1 0.6 copy.83
  (71 shorter events, 3.5 us)
Async XLA Ops:
  0.0 8.3 %copy-start = (bf16[256,1024]{1,0:T(8,128)(2,1)S(1)}, bf16[256,1024]{1,0:T(8,128)(2,1)}, u32[]{:S(2)}) copy-start(bf16[256,1024]{1,0:T(8,128)(2,1)} %param.16) | copy-start | bytes 1572868
  1.4 51.7 %all-to-all-start.1 = ((bf16[1,8,1]{2,0,1:T(2,128)(2,1)}), bf16[1,8,1]{2,0,1:T(2,128)(2,1)S(1)}, u32[]{:S(2)}, u32[]{:S(2)}) async-start(bf16[1,8,1]{2,0,1:T(2,128)(2,1)} %copy.49), calls=%async_computation.1 | async-start | bytes 8192 | tf_op jit(solution)/shard_map/all_to_all | solution.py:149
  6.6 0.7 copy-start.12
  7.3 0.7 copy-start.6
  8.6 0.6 copy-start.7
  9.2 0.7 copy-start.5
  10.1 0.7 copy-start.9
  10.8 0.7 copy-start.11
  21.5 0.7 slice-start
  35.5 0.8 %copy-start.13 = (u32[32]{0:T(128)S(1)}, u32[32]{0:T(128)}, u32[]{:S(2)}) copy-start(u32[32]{0:T(128)} %constant.98) | copy-start | bytes 388
  35.5 0.7 slice-start.1
  35.5 25.7 %copy-start.10 = (bf16[256,1024]{1,0:T(8,128)(2,1)S(1)}, bf16[256,1024]{1,0:T(8,128)(2,1)}, u32[]{:S(2)}) copy-start(bf16[256,1024]{1,0:T(8,128)(2,1)} %param.20) | copy-start | bytes 1572868
  50.0 0.9 %copy-start.3 = (bf16[256,256]{1,0:T(8,128)(2,1)S(1)}, bf16[256,256]{1,0:T(8,128)(2,1)}, u32[]{:S(2)}) copy-start(bf16[256,256]{1,0:T(8,128)(2,1)} %param.17) | copy-start | bytes 393220
  50.3 0.7 %copy-start.8 = (bf16[1,8,1024]{2,1,0:T(8,128)(2,1)S(1)}, bf16[1,8,1024]{2,1,0:T(8,128)(2,1)}, u32[]{:S(2)}) copy-start(bf16[1,8,1024]{2,1,0:T(8,128)(2,1)} %copy-done.7) | copy-start | bytes 49156
  53.1 7.9 %all-to-all-start = ((bf16[8,2,128]{2,1,0:T(2,128)(2,1)}), bf16[8,2,128]{2,1,0:T(2,128)(2,1)S(1)}, u32[]{:S(2)}, u32[]{:S(2)}) async-start(bf16[8,2,128]{2,1,0:T(2,128)(2,1)} %reshape.228), calls=%async_computation | async-start | bytes 8192 | tf_op jit(solution)/shard_map/all_to_all | solution.py:148
  61.3 1.1 %copy-start.4 = (bf16[256,256]{1,0:T(8,128)(2,1)S(1)}, bf16[256,256]{1,0:T(8,128)(2,1)}, u32[]{:S(2)}) copy-start(bf16[256,256]{1,0:T(8,128)(2,1)} %param.21) | copy-start | bytes 393220
  61.3 1.6 %copy-start.2 = (bf16[256,1024]{1,0:T(8,128)(2,1)S(1)}, bf16[256,1024]{1,0:T(8,128)(2,1)}, u32[]{:S(2)}) copy-start(bf16[256,1024]{1,0:T(8,128)(2,1)} %param.22) | copy-start | bytes 1572868
  61.5 1.3 %copy-start.1 = (bf16[1024,256]{1,0:T(8,128)(2,1)S(1)}, bf16[1024,256]{1,0:T(8,128)(2,1)}, u32[]{:S(2)}) copy-start(bf16[1024,256]{1,0:T(8,128)(2,1)} %param.23) | copy-start | bytes 1572868
where the time goes:
time: 72.2 us; the launch traced here: 71.7 us
  blocking collectives  41.9 us (58%)
  local copies, waits for them, and re-layouts  9.98 us (14%)
  starting transfers between devices  8.51 us (12%)
  waiting for transfers between devices  4.3 us (6%)
  other arithmetic  3.88 us (5%)
  matrix products  2.23 us (3%)
  between operations  0.87 us (1%)
    all_gather x1, blocking collectives, body(): lax.all_gather(projected[..., expanded_dimension:3 * expanded_dimension],...  13.4 us
    unnamed x1, blocking collectives  11.7 us
    all_gather x1, blocking collectives, body(): pair_bias = lax.all_gather(local_bias, 'dap', axis=2, tiled=True)  9.75 us
    all_to_all x1, blocking collectives, body(): lax.all_to_all(mixed, 'dap', split_axis=0, concat_axis=1, tiled=True)  7.05 us
    unnamed x37, local copies, waits for them, and re-layouts  7.04 us
    all_to_all x1, starting transfers between devices, body(): lax.all_to_all(keep_blocks, 'dap', split_axis=1, concat_axis=0, tiled=True)  5.2 us
    all_to_all x1, waiting for transfers between devices, body(): lax.all_to_all(blocks, 'dap', split_axis=1, concat_axis=0, tiled=True)  4.3 us
    all_to_all x1, starting transfers between devices, body(): lax.all_to_all(blocks, 'dap', split_axis=1, concat_axis=0, tiled=True)  3.31 us
  transfers between devices with their start and end apart: 2, of which 1 were waited for; matrix products, arithmetic and copies ran while one was open for 8% of the time, Pallas kernels for 0%

commit v1 on v0

--- a/solution.py
+++ b/solution.py
@@ -76,6 +76,18 @@
     expansion_matrix,
     contraction_matrix,
 ):
+
+    def _time_pairs_all(payload):
+        reached, row_out = (lax.axis_size("seq"), lax.axis_index("seq"))
+        now, odd = (payload, 1)
+        while odd < reached:
+            after = lax.ppermute(now, "seq", [(to_i, to_i ^ odd) for to_i in range(reached)])
+            prior = jnp.concatenate([now, after], 1)
+            state_next = jnp.concatenate([after, now], axis=1)
+            now = jnp.where(row_out & odd == 0, prior, state_next)
+            odd = 2 * odd
+        return now
+
     row_count, local_residues, channels = homolog_tensor.shape
     expanded_dimension = HEAD_TOTAL * HEAD_DEPTH
     dap_count = lax.axis_size("dap")
@@ -105,9 +117,7 @@
     queries = projected[..., :expanded_dimension]
     gating = projected[..., 3 * expanded_dimension :]
     key_values, keep_all = (
-        lax.all_gather(
-            projected[..., expanded_dimension : 3 * expanded_dimension], "seq", axis=1, tiled=True
-        ),
+        _time_pairs_all(projected[..., expanded_dimension : 3 * expanded_dimension]),
         lax.all_gather(keep_mask, "seq", axis=1, tiled=True),
     )
 

time: 72.2 us -> 62.2 us (0.86)
  blocking collectives: 41.9 us -> 27.8 us
  waiting for transfers between devices: 4.3 us -> 8.9 us
  local copies, waits for them, and re-layouts: 9.98 us -> 7.72 us
  starting transfers between devices: 8.51 us -> 10.2 us
    all_gather x1 -> x0, blocking collectives: 13.4 us -> none  [body(): lax.all_gather(projected[..., expanded_dimension:3 * expanded_dimension],...]
    ppermute x0 -> x2, waiting for transfers between devices: none -> 4.6 us  [_time_pairs_all(): lax.ppermute(now, 'seq', [(to_i, to_i ^ odd) for to_i in range(reached)])]
    ppermute x0 -> x2, starting transfers between devices: none -> 3.19 us  [_time_pairs_all(): lax.ppermute(now, 'seq', [(to_i, to_i ^ odd) for to_i in range(reached)])]
    unnamed x37 -> x39, local copies, waits for them, and re-layouts: 7.04 us -> 5.25 us
    all_to_all x1, starting transfers between devices: 5.2 us -> 3.72 us  [body(): lax.all_to_all(keep_blocks, 'dap', split_axis=1, concat_axis=0, tiled=True)]
    reduce_sum x3, other arithmetic: 0.31 us -> 1.07 us  [layer_norm(): center = inputs - jnp.mean(inputs, axis=-1, keepdims=True)]
    unnamed x1, blocking collectives: 11.7 us -> 11 us
  transfers between devices with their start and end apart: 2 -> 4, of which waited for: 1 -> 2; matrix products, arithmetic and copies ran while one was open for 8% -> 9% of each run, Pallas kernels for 0% -> 0%
where the time goes in v1:
time: 62.2 us; the launch traced here: 61.7 us
  blocking collectives  27.8 us (45%)
  starting transfers between devices  10.2 us (16%)
  waiting for transfers between devices  8.9 us (14%)
  local copies, waits for them, and re-layouts  7.72 us (12%)
  other arithmetic  3.94 us (6%)
  matrix products  2.23 us (4%)
  between operations  0.94 us (2%)
    unnamed x1, blocking collectives  11 us
    all_gather x1, blocking collectives, body(): pair_bias = lax.all_gather(local_bias, 'dap', axis=2, tiled=True)  9.75 us
    all_to_all x1, blocking collectives, body(): lax.all_to_all(mixed, 'dap', split_axis=0, concat_axis=1, tiled=True)  7.05 us
    unnamed x39, local copies, waits for them, and re-layouts  5.25 us
    ppermute x2, waiting for transfers between devices, _time_pairs_all(): lax.ppermute(now, 'seq', [(to_i, to_i ^ odd) for to_i in range(reached)])  4.6 us
    all_to_all x1, waiting for transfers between devices, body(): lax.all_to_all(blocks, 'dap', split_axis=1, concat_axis=0, tiled=True)  4.3 us
    all_to_all x1, starting transfers between devices, body(): lax.all_to_all(keep_blocks, 'dap', split_axis=1, concat_axis=0, tiled=True)  3.72 us
    all_to_all x1, starting transfers between devices, body(): lax.all_to_all(blocks, 'dap', split_axis=1, concat_axis=0, tiled=True)  3.31 us
  transfers between devices with their start and end apart: 4, of which 2 were waited for; matrix products, arithmetic and copies ran while one was open for 9% of the time, Pallas kernels for 0%

profile of v1, /device:TPU:0, one launch (start us, length us, event | category | flops | bytes accessed | tf_op | source)
XLA Modules:
  0.0 61.7 jit_solution(14862820971729234730)
XLA Ops:
  0.0 0.9 %convert_reduce_fusion.1 = f32[8]{0:T(128)S(1)} fusion(bf16[1,8,256]{2,1,0:T(8,128)(2,1)} %param.12), kind=kLoop, calls=%fused_computation.52 | loop fusion | flops 4088 | bytes 4128 | tf_op jit(solution)/shard_map/reduce_sum | solution.py:12
  0.9 0.2 fusion.38
  1.1 0.2 fusion.12
  1.3 3.1 %collective-permute-start = (bf16[1,8,512]{2,1,0:T(8,128)(2,1)S(1)}, bf16[1,8,512]{2,1,0:T(8,128)(2,1)S(1)}, u32[]{:S(2)}, u32[]{:S(2)}) collective-permute-start(bf16[1,8,512]{2,1,0:T(8,128)(2,1)S(1)} %get-tuple-element.45), channel_id=1, source_target_pairs={{0,1},{1,0},{2,3},{3,2},{4,5},{5,4},{6,7},{7,6},{8,9},{9,8},{10,11... | collective-permute-start | bytes 24584 | tf_op jit(solution)/shard_map/ppermute | solution.py:84
  4.4 0.7 %copy.49 = bf16[1,8,1]{2,0,1:T(2,128)(2,1)} copy(bf16[1,8,1]{1,2,0:T(2,128)(2,1)S(1)} %get-tuple-element.56) | data formatting | bytes 32 | tf_op jit(solution)/shard_map/reshape | solution.py:146
  5.1 3.7 %all-to-all-start.1 = ((bf16[1,8,1]{2,0,1:T(2,128)(2,1)}), bf16[1,8,1]{2,0,1:T(2,128)(2,1)S(1)}, u32[]{:S(2)}, u32[]{:S(2)}) async-start(bf16[1,8,1]{2,0,1:T(2,128)(2,1)} %copy.49), calls=%async_computation.1 | async-start | bytes 8192 | tf_op jit(solution)/shard_map/all_to_all | solution.py:159
  8.9 0.6 %copy-done.13 = s32[32]{0:T(128)S(1)} copy-done((s32[32]{0:T(128)S(1)}, s32[32]{0:T(128)}, u32[]{:S(2)}) %copy-start.13) | copy-done | bytes 152
  10.2 0.6 copy-done.9
  10.8 0.7 %copy-done.14 = u32[32]{0:T(128)S(1)} copy-done((u32[32]{0:T(128)S(1)}, u32[32]{0:T(128)}, u32[]{:S(2)}) %copy-start.14) | copy-done | bytes 152
  11.4 0.6 dynamic-slice
  12.7 0.2 dynamic-update-slice
  12.9 11.0 %all-reduce = bf16[32]{0:T(256)(128)(2,1)S(1)} all-reduce(bf16[32]{0:T(256)(128)(2,1)S(1)} %dynamic-update-slice), channel_id=1, replica_groups=mesh['dap'=8,'seq'=4] {'seq'}, use_global_device_ids=true, to_apply=%add | all-reduce | flops 32 | bytes 128
  24.1 9.7 %all_gather.7 = bf16[8,8,32]{1,0,2:T(8,128)(2,1)S(1)} all-gather(bf16[8,8,4]{1,0,2:T(8,128)(2,1)S(1)} %copy.43), channel_id=1, replica_groups=mesh['dap'=8,'seq'=4] {'dap'}, dimensions={2}, use_global_device_ids=true | all-gather | bytes 4608 | tf_op jit(solution)/shard_map/all_gather | solution.py:108
  34.0 0.7 %slice-done = bf16[1,8,256]{2,1,0:T(8,128)(2,1)S(1)} async-done(((bf16[1,8,1024]{2,1,0:T(8,128)(2,1)}), bf16[1,8,256]{2,1,0:T(8,128)(2,1)S(1)}, s32[]{:S(2)}) %slice-start) | async-done | bytes 4120 | tf_op jit(solution)/shard_map/slice | solution.py:117
  34.9 4.6 %collective-permute-done.1 = bf16[1,16,512]{2,1,0:T(8,128)(2,1)S(1)} collective-permute-done((bf16[1,16,512]{2,1,0:T(8,128)(2,1)S(1)}, bf16[1,16,512]{2,1,0:T(8,128)(2,1)S(1)}, u32[]{:S(2)}, u32[]{:S(2)}) %collective-permute-start.1) | collective-permute-done | bytes 16416 | tf_op jit(solution)/shard_map/ppermute | solution.py:84
  40.0 0.3 convolution_bitcast_fusion.1
  40.4 0.5 copy-done.3
  41.2 0.6 broadcast.233
  41.8 0.7 %reduce.5 = bf16[8,256]{1,0:T(8,128)(2,1)S(1)} reduce(bf16[8,1,1,256]{3,2,1,0:T(2,128)(2,1)S(1)} %bitcast.77, bf16[]{:T(256)} %broadcast.233), dimensions={1,2}, to_apply=%bitcast.76.reduce_sub_computation | reduce | bytes 8194
  42.5 0.6 reshape.311
  43.1 3.3 %all-to-all-start = ((bf16[8,2,128]{2,1,0:T(2,128)(2,1)}), bf16[8,2,128]{2,1,0:T(2,128)(2,1)S(1)}, u32[]{:S(2)}, u32[]{:S(2)}) async-start(bf16[8,2,128]{2,1,0:T(2,128)(2,1)} %reshape.311), calls=%async_computation | async-start | bytes 8192 | tf_op jit(solution)/shard_map/all_to_all | solution.py:158
  46.5 0.2 compare_reduce_fusion
  46.7 4.3 %all-to-all-done = bf16[8,2,128]{2,1,0:T(2,128)(2,1)S(1)} async-done(((bf16[8,2,128]{2,1,0:T(2,128)(2,1)}), bf16[8,2,128]{2,1,0:T(2,128)(2,1)S(1)}, u32[]{:S(2)}, u32[]{:S(2)}) %all-to-all-start) | async-done | bytes 4128 | tf_op jit(solution)/shard_map/all_to_all | solution.py:158
  51.1 0.2 fusion.40
  51.4 0.2 convolution_convert_fusion
  52.1 0.2 convolution_bitcast_fusion
  52.4 0.3 fusion.72
  52.7 0.2 multiply_reduce_fusion
  52.9 0.4 fusion.18
  53.3 0.7 %reduce.6 = bf16[8,256]{1,0:T(8,128)(2,1)S(1)} reduce(bf16[8,1,1,256]{3,0,2,1:T(8,128)(2,1)S(1)} %fusion.18, bf16[]{:T(256)} %broadcast.233), dimensions={1,2}, to_apply=%copy.55.reduce_sub_computation | reduce | bytes 8194 | tf_op jit(solution)/shard_map/broadcast_in_dim;transpose | solution.py:162
  54.1 7.1 %all_to_all.12 = bf16[8,2,128]{2,1,0:T(2,128)(2,1)S(1)} all-to-all(bf16[8,2,128]{2,1,0:T(2,128)(2,1)S(1)} %reshape.313), channel_id=1, replica_groups=mesh['dap'=8,'seq'=4] {'dap'}, dimensions={0} | all-to-all | bytes 8192 | tf_op jit(solution)/shard_map/all_to_all | solution.py:163
  61.1 0.6 copy.83
  (78 shorter events, 2.9 us)
Async XLA Ops:
  0.0 1.1 %copy-start = (bf16[256,1024]{1,0:T(8,128)(2,1)S(1)}, bf16[256,1024]{1,0:T(8,128)(2,1)}, u32[]{:S(2)}) copy-start(bf16[256,1024]{1,0:T(8,128)(2,1)} %param.16) | copy-start | bytes 1572868
  0.0 0.9 %copy-start.6 = (bf16[1,8,256]{2,1,0:T(8,128)(2,1)S(1)}, bf16[1,8,256]{2,1,0:T(8,128)(2,1)}, u32[]{:S(2)}) copy-start(bf16[1,8,256]{2,1,0:T(8,128)(2,1)} %param.12) | copy-start | bytes 12292
  1.3 22.7 %copy-start.7 = (bf16[1,8,1024]{2,1,0:T(8,128)(2,1)}, bf16[1,8,1024]{2,1,0:T(8,128)(2,1)S(1)}, u32[]{:S(2)}) copy-start(bf16[1,8,1024]{2,1,0:T(8,128)(2,1)S(1)} %fusion.12) | copy-start | bytes 49156
  1.3 3.1 %copy-start.12 = (s32[1,8]{1,0:T(1,128)S(1)}, s32[1,8]{1,0:T(1,128)}, u32[]{:S(2)}) copy-start(s32[1,8]{1,0:T(1,128)} %param.14) | copy-start | bytes 100
  1.3 33.4 %collective-permute-start = (bf16[1,8,512]{2,1,0:T(8,128)(2,1)S(1)}, bf16[1,8,512]{2,1,0:T(8,128)(2,1)S(1)}, u32[]{:S(2)}, u32[]{:S(2)}) collective-permute-start(bf16[1,8,512]{2,1,0:T(8,128)(2,1)S(1)} %get-tuple-element.45), channel_id=1, source_target_pairs={{0,1},{1,0},{2,3},{3,2},{4,5},{5,4},{6,7},{7,6},{8,9},{9,8},{10,11... | collective-permute-start | bytes 24584 | tf_op jit(solution)/shard_map/ppermute | solution.py:84
  5.1 38.0 %all-to-all-start.1 = ((bf16[1,8,1]{2,0,1:T(2,128)(2,1)}), bf16[1,8,1]{2,0,1:T(2,128)(2,1)S(1)}, u32[]{:S(2)}, u32[]{:S(2)}) async-start(bf16[1,8,1]{2,0,1:T(2,128)(2,1)} %copy.49), calls=%async_computation.1 | async-start | bytes 8192 | tf_op jit(solution)/shard_map/all_to_all | solution.py:159
  8.8 0.7 %copy-start.13 = (s32[32]{0:T(128)S(1)}, s32[32]{0:T(128)}, u32[]{:S(2)}) copy-start(s32[32]{0:T(128)} %param.15) | copy-start | bytes 388
  8.8 0.9 %copy-start.5 = (bf16[8,4,128]{2,1,0:T(4,128)(2,1)S(1)}, bf16[8,4,128]{2,1,0:T(4,128)(2,1)}, u32[]{:S(2)}) copy-start(bf16[8,4,128]{2,1,0:T(4,128)(2,1)} %param.13) | copy-start | bytes 24580
  10.1 0.7 %copy-start.9 = (f32[2,8]{1,0:T(2,128)S(1)}, f32[2,8]{1,0:T(2,128)}, u32[]{:S(2)}) copy-start(f32[2,8]{1,0:T(2,128)} %param.19) | copy-start | bytes 196
  10.7 0.7 %copy-start.14 = (u32[32]{0:T(128)S(1)}, u32[32]{0:T(128)}, u32[]{:S(2)}) copy-start(u32[32]{0:T(128)} %constant.102) | copy-start | bytes 388
  12.6 11.2 %copy-start.11 = (f32[128,8]{0,1:T(8,128)S(1)}, f32[128,8]{0,1:T(8,128)}, u32[]{:S(2)}) copy-start(f32[128,8]{0,1:T(8,128)} %param.18) | copy-start | bytes 12292
  34.0 0.7 %slice-start = ((bf16[1,8,1024]{2,1,0:T(8,128)(2,1)}), bf16[1,8,256]{2,1,0:T(8,128)(2,1)S(1)}, s32[]{:S(2)}) async-start(bf16[1,8,1024]{2,1,0:T(8,128)(2,1)} %copy-done.7), calls=%async_computation.3 | async-start | bytes 8192 | tf_op jit(solution)/shard_map/slice | solution.py:117
  34.8 4.7 %collective-permute-start.1 = (bf16[1,16,512]{2,1,0:T(8,128)(2,1)S(1)}, bf16[1,16,512]{2,1,0:T(8,128)(2,1)S(1)}, u32[]{:S(2)}, u32[]{:S(2)}) collective-permute-start(bf16[1,16,512]{2,1,0:T(8,128)(2,1)S(1)} %maximum_select_fusion.2), channel_id=1, source_target_pairs={{0,2},{1,3},{2,0},{3,1},{4,6},{5,7},{6,4},{7,5},{8,10},{9,11},{10,... | collective-permute-start | bytes 49160 | tf_op jit(solution)/shard_map/ppermute | solution.py:84
  34.9 16.5 %copy-start.10 = (bf16[256,1024]{1,0:T(8,128)(2,1)S(1)}, bf16[256,1024]{1,0:T(8,128)(2,1)}, u32[]{:S(2)}) copy-start(bf16[256,1024]{1,0:T(8,128)(2,1)} %param.20) | copy-start | bytes 1572868
  40.0 0.9 %copy-start.3 = (bf16[256,256]{1,0:T(8,128)(2,1)S(1)}, bf16[256,256]{1,0:T(8,128)(2,1)}, u32[]{:S(2)}) copy-start(bf16[256,256]{1,0:T(8,128)(2,1)} %param.17) | copy-start | bytes 393220
  40.3 0.7 %copy-start.8 = (bf16[1,8,1024]{2,1,0:T(8,128)(2,1)S(1)}, bf16[1,8,1024]{2,1,0:T(8,128)(2,1)}, u32[]{:S(2)}) copy-start(bf16[1,8,1024]{2,1,0:T(8,128)(2,1)} %copy-done.7) | copy-start | bytes 49156
  43.1 7.9 %all-to-all-start = ((bf16[8,2,128]{2,1,0:T(2,128)(2,1)}), bf16[8,2,128]{2,1,0:T(2,128)(2,1)S(1)}, u32[]{:S(2)}, u32[]{:S(2)}) async-start(bf16[8,2,128]{2,1,0:T(2,128)(2,1)} %reshape.311), calls=%async_computation | async-start | bytes 8192 | tf_op jit(solution)/shard_map/all_to_all | solution.py:158
  51.3 1.1 %copy-start.4 = (bf16[256,256]{1,0:T(8,128)(2,1)S(1)}, bf16[256,256]{1,0:T(8,128)(2,1)}, u32[]{:S(2)}) copy-start(bf16[256,256]{1,0:T(8,128)(2,1)} %param.21) | copy-start | bytes 393220
  51.4 1.6 %copy-start.2 = (bf16[256,1024]{1,0:T(8,128)(2,1)S(1)}, bf16[256,1024]{1,0:T(8,128)(2,1)}, u32[]{:S(2)}) copy-start(bf16[256,1024]{1,0:T(8,128)(2,1)} %param.22) | copy-start | bytes 1572868
  51.6 1.3 %copy-start.1 = (bf16[1024,256]{1,0:T(8,128)(2,1)S(1)}, bf16[1024,256]{1,0:T(8,128)(2,1)}, u32[]{:S(2)}) copy-start(bf16[1024,256]{1,0:T(8,128)(2,1)} %param.23) | copy-start | bytes 1572868
